TPU v7x, 512 devices: a whole 4x4x16 slice. The times are simulated.
512 devices in a mesh: dp: 32 (over z, core), seq: 16 (over y, x).
Axes of the slice: x: 4, y: 4, z: 16, core: 2. Of those that a mesh axis runs over, the one named last changes fastest.
Arguments:
- features: bfloat16 [32, 3072, 1024], P('dp', 'seq'), may hold values from -18 to 18
- qkv_weight: bfloat16 [1024, 3072], P('dp'), may hold values from -1 to 1
- cotangent: bfloat16 [32, 3072, 1024], P('dp', 'seq'), may hold values from -6 to 6
- node_order: int32 [32, 3072], P('dp'), may hold values from 0 to 3071, as said below
- blocks: int32 [32, 48, 8], P('dp'), may hold values from 0 to 47, as said below
- counts: int32 [32, 48], P('dp'), may hold values from 1 to 8, as said below
Outputs:
- attended: bfloat16 [32, 3072, 1024], P('dp', 'seq')
- grad_features: bfloat16 [32, 3072, 1024], P('dp', 'seq')
- grad_weight: float32 [1024, 3072], P('dp', 'seq')
Inputs may be any that keep to these rules, and one draw needn't show every extreme that they name: Every row of node_order lists each node of the subgraph once. blocks[g, c, 0] is c, and the 8 entries of a row are distinct clusters; slots at or beyond counts[g, c] are unused. `counts`: every subgraph has a cluster with all 8 slots live.
All inputs are finite; a program needn't handle non-finite values.
Results may differ from a plain program's by a relative error of at most 0.03.
Values may be sent and summed in bfloat16 or wider, within the bound.
No kernel may reach another device: no remote copies, remote signals or barrier semaphores. Data moves between devices by JAX's collectives and lax.ppermute only.
A program may use at most 128 MiB of HBM per device.

v0:
```python
import math
import jax
import jax.numpy as jnp
from jax import lax
from jax.sharding import PartitionSpec as P

HEADS = 16
HD = 64


def attend(query, key_in, value, grad_out, blocks, counts):
    cluster_count, slot_count = blocks.shape
    node_count, head_width = query.shape
    block_rows = node_count // cluster_count
    in_group = math.gcd(cluster_count, 8)
    runs_total = cluster_count // in_group
    score_scale = 1.0 / math.sqrt(head_width)
    key_blocks = key_in.reshape(cluster_count, block_rows, head_width)
    value_blocks = value.reshape(cluster_count, block_rows, head_width)
    inputs_all = (
        query.reshape(runs_total, in_group, block_rows, head_width),
        grad_out.reshape(runs_total, in_group, block_rows, head_width),
        blocks.reshape(runs_total, in_group, slot_count),
        counts.reshape(runs_total, in_group),
    )

    def group_step(totals, inputs_now):
        grad_key, grad_value = totals
        query_block, grad_block, block_ids, live_count = inputs_now
        key_rows = key_blocks[block_ids].reshape(in_group, slot_count * block_rows, head_width)
        value_rows = value_blocks[block_ids].reshape(in_group, slot_count * block_rows, head_width)
        is_live = jnp.repeat(
            jnp.arange(slot_count)[None, :] < live_count[:, None], block_rows, axis=1
        )[:, None, :]
        scores = (
            jnp.einsum("cqe,cke->cqk", query_block, key_rows, preferred_element_type=jnp.float32)
            * score_scale
        )
        scores = jnp.where(is_live, scores, -1e30)
        row_max = jnp.max(scores, axis=-1, keepdims=True)
        raw_weights = jnp.where(is_live, jnp.exp(scores - row_max), 0.0)
        attn_weights = raw_weights / jnp.sum(raw_weights, axis=-1, keepdims=True)
        attn_low = attn_weights.astype(jnp.bfloat16)
        output_blk = jnp.einsum(
            "cqk,cke->cqe", attn_low, value_rows, preferred_element_type=jnp.float32
        ).astype(jnp.bfloat16)
        grad_weights = jnp.einsum(
            "cqe,cke->cqk", grad_block, value_rows, preferred_element_type=jnp.float32
        )
        row_dot = jnp.sum(attn_weights * grad_weights, axis=-1, keepdims=True)
        grad_scores = (attn_weights * (grad_weights - row_dot) * score_scale).astype(jnp.bfloat16)
        grad_query = jnp.einsum(
            "cqk,cke->cqe", grad_scores, key_rows, preferred_element_type=jnp.float32
        ).astype(jnp.bfloat16)
        key_terms = jnp.einsum(
            "cqk,cqe->cke", grad_scores, query_block, preferred_element_type=jnp.float32
        )
        value_terms = jnp.einsum(
            "cqk,cqe->cke", attn_low, grad_block, preferred_element_type=jnp.float32
        )
        grad_key = grad_key.at[block_ids].add(
            key_terms.reshape(in_group, slot_count, block_rows, head_width)
        )
        grad_value = grad_value.at[block_ids].add(
            value_terms.reshape(in_group, slot_count, block_rows, head_width)
        )
        return ((grad_key, grad_value), (output_blk, grad_query))

    empty_sum = jnp.zeros((cluster_count, block_rows, head_width), jnp.float32)
    (grad_key, grad_value), (output_all, grad_query) = lax.scan(
        group_step, (empty_sum, empty_sum), inputs_all
    )
    return (
        output_all.reshape(node_count, head_width),
        grad_query.reshape(node_count, head_width),
        grad_key.reshape(node_count, head_width).astype(jnp.bfloat16),
        grad_value.reshape(node_count, head_width).astype(jnp.bfloat16),
    )


def per_device(features, qkv_weight, cotangent, node_order, blocks, counts):
    local_rows = features.shape[1]
    model_width = features.shape[2]
    heads_local = HEADS // lax.axis_size("seq")
    three_width = 3 * HD
    node_feats = features[0]
    cot_heads = cotangent[0].reshape(local_rows, HEADS, HD)
    weights_all = lax.all_gather(qkv_weight, "dp", axis=0, tiled=True)
    node_all = lax.all_gather(node_feats, "seq", axis=0, tiled=True)
    node_count = node_all.shape[0]
    projected = jnp.dot(node_feats, weights_all, preferred_element_type=jnp.float32).astype(
        jnp.bfloat16
    )
    projected = projected.reshape(local_rows, HEADS, three_width)
    head_qkv, head_cot = (
        lax.all_to_all(projected, "seq", split_axis=1, concat_axis=0, tiled=True),
        lax.all_to_all(cot_heads, "seq", split_axis=1, concat_axis=0, tiled=True),
    )
    graph_order = node_order[0]
    inverse = (
        jnp.zeros((node_count,), jnp.int32)
        .at[graph_order]
        .set(jnp.arange(node_count, dtype=jnp.int32))
    )
    sorted_qkv = head_qkv[graph_order]
    sorted_cot = head_cot[graph_order]
    output_all, grad_query, grad_key, grad_value = jax.vmap(
        attend, in_axes=(1, 1, 1, 1, None, None), out_axes=1
    )(
        sorted_qkv[:, :, :HD],
        sorted_qkv[:, :, HD : 2 * HD],
        sorted_qkv[:, :, 2 * HD :],
        sorted_cot,
        blocks[0],
        counts[0],
    )
    grad_heads = jnp.concatenate([grad_query, grad_key, grad_value], axis=-1)[inverse]
    output_nodes = output_all[inverse]
    output_back, grad_back = (
        lax.all_to_all(output_nodes, "seq", split_axis=0, concat_axis=1, tiled=True),
        lax.all_to_all(grad_heads, "seq", split_axis=0, concat_axis=1, tiled=True),
    )
    attended = output_back.reshape(1, local_rows, model_width)
    grad_local = grad_back.reshape(local_rows, 3 * model_width)
    grad_feats = lax.dot_general(
        grad_local, weights_all, (((1,), (1,)), ((), ())), preferred_element_type=jnp.float32
    )
    grad_features = grad_feats.astype(jnp.bfloat16).reshape(1, local_rows, model_width)
    head_grads = grad_heads.reshape(node_count, heads_local * three_width)
    grad_weight = lax.psum_scatter(
        lax.dot_general(
            node_all, head_grads, (((0,), (0,)), ((), ())), preferred_element_type=jnp.float32
        ).astype(jnp.bfloat16),
        "dp",
        scatter_dimension=0,
        tiled=True,
    ).astype(jnp.float32)
    return (attended, grad_features, grad_weight)


def solution(mesh):
    return jax.shard_map(
        per_device,
        mesh=mesh,
        in_specs=(
            P("dp", "seq", None),
            P("dp", None),
            P("dp", "seq", None),
            P("dp", None),
            P("dp", None, None),
            P("dp", None),
        ),
        out_specs=(P("dp", "seq", None), P("dp", "seq", None), P("dp", "seq")),
        check_vma=False,
    )
```

profile of v0, /device:TPU:8, one launch (start us, length us, event | category | flops | bytes accessed | tf_op | source)
XLA Modules:
  0.0 628.1 jit_solution(6024842970168261089)
XLA Ops:
  9.9 9.2 %all-to-all-start.1 = ((bf16[192,16,64]{0,2,1:T(8,128)(2,1)}), bf16[192,16,64]{0,2,1:T(8,128)(2,1)S(1)}, u32[]{:S(2)}, u32[]{:S(2)}) async-start(bf16[192,16,64]{0,2,1:T(8,128)(2,1)} %bitcast.27), calls=%async_computation.1 | async-start | bytes 1048576 | tf_op jit(solution)/shard_map/all_to_all | solution.py:97
  21.2 70.2 %all-gather.4.cloned.1.call-done = bf16[1024,3072]{1,0:T(8,128)(2,1)} async-done(((bf16[32,3072]{1,0:T(8,128)(2,1)}), bf16[1024,3072]{1,0:T(8,128)(2,1)}) %all-gather.4.cloned.1.call-update) | async-done | bytes 6291472 | tf_op jit(solution)/shard_map/all_gather | solution.py:88
  91.5 5.3 convolution_convert_fusion.2
  96.7 3.0 reshape.196
  101.5 7.4 %all-to-all-start = ((bf16[192,16,192]{2,0,1:T(8,128)(2,1)}), bf16[192,16,192]{2,0,1:T(8,128)(2,1)S(1)}, u32[]{:S(2)}, u32[]{:S(2)}) async-start(bf16[192,16,192]{2,0,1:T(8,128)(2,1)} %copy.93), calls=%async_computation | async-start | bytes 3145728 | tf_op jit(solution)/shard_map/all_to_all | solution.py:96
  108.9 12.0 %scatter_custom_fusion.2 = s32[3072]{0:T(1024)S(1)} fusion(s32[3072]{0:T(1024)S(1)} %bitcast.182, s32[3072]{0:T(1024)S(1)} %iota.7, s32[]{:T(128)} %copy.139), kind=kCustom, calls=%fused_computation.71 | custom fusion | bytes 12292 | tf_op jit(solution)/shard_map/scatter | solution.py:103
  121.3 11.4 %gather_fusion.3 = bf16[3072,64]{1,0:T(8,128)(2,1)} fusion(bf16[3072,64]{1,0:T(8,128)(2,1)S(1)} %bitcast.161, s32[3072]{0:T(1024)S(1)} %broadcast_clamp_fusion), kind=kCustom, calls=%fused_computation.3 | custom fusion | bytes 798720 | tf_op jit(solution)/shard_map/gather | solution.py:106
  132.7 4.4 all-to-all-done
  137.2 11.1 %gather_fusion.2 = bf16[3072,192]{1,0:T(8,128)(2,1)S(1)} fusion(bf16[3072,192]{1,0:T(8,128)(2,1)S(1)} %bitcast.152, s32[3072]{0:T(1024)S(1)} %broadcast_clamp_fusion), kind=kCustom, calls=%fused_computation.2 | custom fusion | bytes 2371584 | tf_op jit(solution)/shard_map/gather | solution.py:105
  150.4 286.3 %while.16 = (s32[]{:T(128)}, f32[1,48,64,64]{3,2,1,0:T(8,128)S(1)}, f32[1,48,64,64]{3,2,1,0:T(8,128)S(1)}, bf16[6,1,8,64,64]{4,3,2,1,0:T(8,128)(2,1)}, bf16[6,1,...) while((s32[]{:T(128)}, f32[1,48,64,64]{3,2,1,0:T(8,128)S(1)}, ...), condition=%wide.region_6.7_spmd, body=%wide.region_0.6_spmd.sunk | while | flops 209000192 | bytes 36499064 | solution.py:70
  150.5 2.9 gather_fusion.1
  157.6 2.8 gather_fusion
  160.5 2.8 fusion.106
  163.3 6.0 fusion.113
  169.3 4.3 fusion.111
  173.6 7.0 %scatter_fusion.1 = f32[48,64,64]{2,1,0:T(8,128)S(1)} fusion(f32[48,64,64]{2,1,0:T(8,128)S(1)} %bitcast.155, s32[64]{0:T(128)S(1)} %reshape.343, f32[64,64,64]{2,1,0:T(8,128)} %bitcast.163), kind=kCustom, calls=%fused_computation.7.clone.1 | custom fusion | flops 262144 | bytes 3145984 | tf_op jit(solution)/shard_map/vmap()/while/body/eval_jaxpr/scatter-add | solution.py:64
  180.6 7.0 %fusion.110 = f32[8,512,64]{2,1,0:T(8,128)} fusion(f32[8,64,512]{2,1,0:T(8,128)} %fusion.106, bf16[6,1,8,64,64]{4,3,2,1,0:T(8,128)(2,1)} %get-tuple-element.266, s32[]{:T(128)} %get-tuple-element.247, f32[8,64,512]{2,1,0:T(8,128)} %get-tuple-element.233, f32[8,64]{1,0:T(8,128)S(1)} %get-tuple-element.234), kind=kOutput, calls=%fused_computation.26.clone.1 | convolution fusion | flops 35390464 | bytes 5382656 | tf_op jit(solution)/shard_map/vmap()/while/body/eval_jaxpr/reshape | solution.py:62
  187.7 7.0 %scatter_fusion = f32[48,64,64]{2,1,0:T(8,128)S(1)} fusion(f32[48,64,64]{2,1,0:T(8,128)S(1)} %bitcast.153, s32[64]{0:T(128)S(1)} %reshape.343, f32[64,64,64]{2,1,0:T(8,128)} %bitcast.162), kind=kCustom, calls=%fused_computation.6.clone.1 | custom fusion | flops 262144 | bytes 3145984 | tf_op jit(solution)/shard_map/vmap()/while/body/eval_jaxpr/scatter-add | solution.py:61
  194.7 3.5 fusion.112
  198.3 2.9 gather_fusion.1
  211.0 6.0 fusion.113
  217.1 4.3 fusion.111
  221.3 7.0 %scatter_fusion.1 = f32[48,64,64]{2,1,0:T(8,128)S(1)} fusion(f32[48,64,64]{2,1,0:T(8,128)S(1)} %bitcast.155, s32[64]{0:T(128)S(1)} %reshape.343, f32[64,64,64]{2,1,0:T(8,128)} %bitcast.163), kind=kCustom, calls=%fused_computation.7.clone.1 | custom fusion | flops 262144 | bytes 3145984 | tf_op jit(solution)/shard_map/vmap()/while/body/eval_jaxpr/scatter-add | solution.py:64
  228.3 7.0 %fusion.110 = f32[8,512,64]{2,1,0:T(8,128)} fusion(f32[8,64,512]{2,1,0:T(8,128)} %fusion.106, bf16[6,1,8,64,64]{4,3,2,1,0:T(8,128)(2,1)} %get-tuple-element.266, s32[]{:T(128)} %get-tuple-element.247, f32[8,64,512]{2,1,0:T(8,128)} %get-tuple-element.233, f32[8,64]{1,0:T(8,128)S(1)} %get-tuple-element.234), kind=kOutput, calls=%fused_computation.26.clone.1 | convolution fusion | flops 35390464 | bytes 5382656 | tf_op jit(solution)/shard_map/vmap()/while/body/eval_jaxpr/reshape | solution.py:62
  235.4 7.0 %scatter_fusion = f32[48,64,64]{2,1,0:T(8,128)S(1)} fusion(f32[48,64,64]{2,1,0:T(8,128)S(1)} %bitcast.153, s32[64]{0:T(128)S(1)} %reshape.343, f32[64,64,64]{2,1,0:T(8,128)} %bitcast.162), kind=kCustom, calls=%fused_computation.6.clone.1 | custom fusion | flops 262144 | bytes 3145984 | tf_op jit(solution)/shard_map/vmap()/while/body/eval_jaxpr/scatter-add | solution.py:61
  242.4 3.5 fusion.112
  246.0 2.9 gather_fusion.1
  258.8 6.0 fusion.113
  264.8 4.3 fusion.111
  269.0 7.0 %scatter_fusion.1 = f32[48,64,64]{2,1,0:T(8,128)S(1)} fusion(f32[48,64,64]{2,1,0:T(8,128)S(1)} %bitcast.155, s32[64]{0:T(128)S(1)} %reshape.343, f32[64,64,64]{2,1,0:T(8,128)} %bitcast.163), kind=kCustom, calls=%fused_computation.7.clone.1 | custom fusion | flops 262144 | bytes 3145984 | tf_op jit(solution)/shard_map/vmap()/while/body/eval_jaxpr/scatter-add | solution.py:64
  276.0 7.0 %fusion.110 = f32[8,512,64]{2,1,0:T(8,128)} fusion(f32[8,64,512]{2,1,0:T(8,128)} %fusion.106, bf16[6,1,8,64,64]{4,3,2,1,0:T(8,128)(2,1)} %get-tuple-element.266, s32[]{:T(128)} %get-tuple-element.247, f32[8,64,512]{2,1,0:T(8,128)} %get-tuple-element.233, f32[8,64]{1,0:T(8,128)S(1)} %get-tuple-element.234), kind=kOutput, calls=%fused_computation.26.clone.1 | convolution fusion | flops 35390464 | bytes 5382656 | tf_op jit(solution)/shard_map/vmap()/while/body/eval_jaxpr/reshape | solution.py:62
  283.1 7.0 %scatter_fusion = f32[48,64,64]{2,1,0:T(8,128)S(1)} fusion(f32[48,64,64]{2,1,0:T(8,128)S(1)} %bitcast.153, s32[64]{0:T(128)S(1)} %reshape.343, f32[64,64,64]{2,1,0:T(8,128)} %bitcast.162), kind=kCustom, calls=%fused_computation.6.clone.1 | custom fusion | flops 262144 | bytes 3145984 | tf_op jit(solution)/shard_map/vmap()/while/body/eval_jaxpr/scatter-add | solution.py:61
  290.1 3.5 fusion.112
  293.7 2.9 gather_fusion.1
  306.5 6.0 fusion.113
  312.5 4.3 fusion.111
  316.7 7.0 %scatter_fusion.1 = f32[48,64,64]{2,1,0:T(8,128)S(1)} fusion(f32[48,64,64]{2,1,0:T(8,128)S(1)} %bitcast.155, s32[64]{0:T(128)S(1)} %reshape.343, f32[64,64,64]{2,1,0:T(8,128)} %bitcast.163), kind=kCustom, calls=%fused_computation.7.clone.1 | custom fusion | flops 262144 | bytes 3145984 | tf_op jit(solution)/shard_map/vmap()/while/body/eval_jaxpr/scatter-add | solution.py:64
  323.8 7.0 %fusion.110 = f32[8,512,64]{2,1,0:T(8,128)} fusion(f32[8,64,512]{2,1,0:T(8,128)} %fusion.106, bf16[6,1,8,64,64]{4,3,2,1,0:T(8,128)(2,1)} %get-tuple-element.266, s32[]{:T(128)} %get-tuple-element.247, f32[8,64,512]{2,1,0:T(8,128)} %get-tuple-element.233, f32[8,64]{1,0:T(8,128)S(1)} %get-tuple-element.234), kind=kOutput, calls=%fused_computation.26.clone.1 | convolution fusion | flops 35390464 | bytes 5382656 | tf_op jit(solution)/shard_map/vmap()/while/body/eval_jaxpr/reshape | solution.py:62
  330.8 7.0 %scatter_fusion = f32[48,64,64]{2,1,0:T(8,128)S(1)} fusion(f32[48,64,64]{2,1,0:T(8,128)S(1)} %bitcast.153, s32[64]{0:T(128)S(1)} %reshape.343, f32[64,64,64]{2,1,0:T(8,128)} %bitcast.162), kind=kCustom, calls=%fused_computation.6.clone.1 | custom fusion | flops 262144 | bytes 3145984 | tf_op jit(solution)/shard_map/vmap()/while/body/eval_jaxpr/scatter-add | solution.py:61
  337.8 3.5 fusion.112
  341.4 2.9 gather_fusion.1
  354.2 6.0 fusion.113
  360.2 4.3 fusion.111
  364.4 7.0 %scatter_fusion.1 = f32[48,64,64]{2,1,0:T(8,128)S(1)} fusion(f32[48,64,64]{2,1,0:T(8,128)S(1)} %bitcast.155, s32[64]{0:T(128)S(1)} %reshape.343, f32[64,64,64]{2,1,0:T(8,128)} %bitcast.163), kind=kCustom, calls=%fused_computation.7.clone.1 | custom fusion | flops 262144 | bytes 3145984 | tf_op jit(solution)/shard_map/vmap()/while/body/eval_jaxpr/scatter-add | solution.py:64
  371.5 7.0 %fusion.110 = f32[8,512,64]{2,1,0:T(8,128)} fusion(f32[8,64,512]{2,1,0:T(8,128)} %fusion.106, bf16[6,1,8,64,64]{4,3,2,1,0:T(8,128)(2,1)} %get-tuple-element.266, s32[]{:T(128)} %get-tuple-element.247, f32[8,64,512]{2,1,0:T(8,128)} %get-tuple-element.233, f32[8,64]{1,0:T(8,128)S(1)} %get-tuple-element.234), kind=kOutput, calls=%fused_computation.26.clone.1 | convolution fusion | flops 35390464 | bytes 5382656 | tf_op jit(solution)/shard_map/vmap()/while/body/eval_jaxpr/reshape | solution.py:62
  378.5 7.0 %scatter_fusion = f32[48,64,64]{2,1,0:T(8,128)S(1)} fusion(f32[48,64,64]{2,1,0:T(8,128)S(1)} %bitcast.153, s32[64]{0:T(128)S(1)} %reshape.343, f32[64,64,64]{2,1,0:T(8,128)} %bitcast.162), kind=kCustom, calls=%fused_computation.6.clone.1 | custom fusion | flops 262144 | bytes 3145984 | tf_op jit(solution)/shard_map/vmap()/while/body/eval_jaxpr/scatter-add | solution.py:61
  385.5 3.5 fusion.112
  389.1 2.9 gather_fusion.1
  401.9 6.0 fusion.113
  407.9 4.3 fusion.111
  412.2 7.0 %scatter_fusion.1 = f32[48,64,64]{2,1,0:T(8,128)S(1)} fusion(f32[48,64,64]{2,1,0:T(8,128)S(1)} %bitcast.155, s32[64]{0:T(128)S(1)} %reshape.343, f32[64,64,64]{2,1,0:T(8,128)} %bitcast.163), kind=kCustom, calls=%fused_computation.7.clone.1 | custom fusion | flops 262144 | bytes 3145984 | tf_op jit(solution)/shard_map/vmap()/while/body/eval_jaxpr/scatter-add | solution.py:64
  419.2 7.0 %fusion.110 = f32[8,512,64]{2,1,0:T(8,128)} fusion(f32[8,64,512]{2,1,0:T(8,128)} %fusion.106, bf16[6,1,8,64,64]{4,3,2,1,0:T(8,128)(2,1)} %get-tuple-element.266, s32[]{:T(128)} %get-tuple-element.247, f32[8,64,512]{2,1,0:T(8,128)} %get-tuple-element.233, f32[8,64]{1,0:T(8,128)S(1)} %get-tuple-element.234), kind=kOutput, calls=%fused_computation.26.clone.1 | convolution fusion | flops 35390464 | bytes 5382656 | tf_op jit(solution)/shard_map/vmap()/while/body/eval_jaxpr/reshape | solution.py:62
  426.2 7.0 %scatter_fusion = f32[48,64,64]{2,1,0:T(8,128)S(1)} fusion(f32[48,64,64]{2,1,0:T(8,128)S(1)} %bitcast.153, s32[64]{0:T(128)S(1)} %reshape.343, f32[64,64,64]{2,1,0:T(8,128)} %bitcast.162), kind=kCustom, calls=%fused_computation.6.clone.1 | custom fusion | flops 262144 | bytes 3145984 | tf_op jit(solution)/shard_map/vmap()/while/body/eval_jaxpr/scatter-add | solution.py:61
  433.2 3.5 fusion.112
  438.9 9.2 %gather_fusion.4 = bf16[3072,64]{1,0:T(8,128)(2,1)S(1)} fusion(bf16[3072,64]{1,0:T(8,128)(2,1)S(1)} %bitcast.164, s32[3072]{0:T(1024)S(1)} %fusion.52), kind=kCustom, calls=%fused_computation.4 | custom fusion | bytes 798720 | tf_op jit(solution)/shard_map/gather | solution.py:118
  451.4 5.9 all-to-all-start.2
  459.1 11.1 %gather_fusion.5 = bf16[3072,192]{1,0:T(8,128)(2,1)S(1)} fusion(bf16[3072,192]{1,0:T(8,128)(2,1)S(1)} %maximum_bitcast_fusion, s32[3072]{0:T(1024)S(1)} %fusion.52), kind=kCustom, calls=%fused_computation.5 | custom fusion | bytes 2371584 | tf_op jit(solution)/shard_map/gather | solution.py:117
  474.5 7.3 %all-to-all-start.3 = ((bf16[16,2,18432]{2,1,0:T(2,128)(2,1)}), bf16[16,2,18432]{2,1,0:T(2,128)(2,1)}, u32[]{:S(2)}, u32[]{:S(2)}) async-start(bf16[16,2,18432]{2,1,0:T(2,128)(2,1)} %reshape.324), calls=%async_computation.3 | async-start | bytes 2359296 | tf_op jit(solution)/shard_map/all_to_all | solution.py:121
  481.8 4.2 fusion.48
  491.1 101.6 %reduce-scatter.4.cloned.1.call-done = bf16[32,192]{1,0:T(8,128)(2,1)} async-done(((bf16[1024,192]{1,0:T(8,128)(2,1)}), bf16[32,192]{1,0:T(8,128)(2,1)}) %reduce-scatter.4.cloned.1.call-update) | async-done | bytes 12304
  594.2 8.4 %reshape.325 = bf16[3072,1,192]{2,1,0:T(2,128)(2,1)S(1)} reshape(bf16[16,2,18432]{2,1,0:T(2,128)(2,1)} %all-to-all-done.3) | data formatting | bytes 2359296
  602.6 6.2 copy.102
  608.7 3.0 all_to_all.60
  615.8 5.7 fusion.47
  (132 shorter events, 85.6 us)
Async XLA Ops:
  7.2 84.3 %copy-start.3 = (bf16[1,192,1024]{2,1,0:T(8,128)(2,1)S(1)}, bf16[1,192,1024]{2,1,0:T(8,128)(2,1)}, u32[]{:S(2)}) copy-start(bf16[1,192,1024]{2,1,0:T(8,128)(2,1)} %param.8) | copy-start | bytes 1179652
  7.2 12.7 %copy-start.5 = (s32[1,48,8]{1,2,0:T(8,128)S(1)}, s32[1,48,8]{1,2,0:T(8,128)}, u32[]{:S(2)}) copy-start(s32[1,48,8]{1,2,0:T(8,128)} %param.12) | copy-start | bytes 4612
  7.2 13.3 %copy-start.6 = (s32[1,48]{1,0:T(1,128)S(1)}, s32[1,48]{1,0:T(1,128)}, u32[]{:S(2)}) copy-start(s32[1,48]{1,0:T(1,128)} %param.13) | copy-start | bytes 580
  7.2 84.3 %all-gather.4.cloned.1.call-start = ((), (), s32[]{:S(2)}) async-start(), calls=%async_computation.5 | async-start | bytes 6488064 | tf_op jit(solution)/shard_map/all_gather | solution.py:88
  9.9 91.6 %all-to-all-start.1 = ((bf16[192,16,64]{0,2,1:T(8,128)(2,1)}), bf16[192,16,64]{0,2,1:T(8,128)(2,1)S(1)}, u32[]{:S(2)}, u32[]{:S(2)}) async-start(bf16[192,16,64]{0,2,1:T(8,128)(2,1)} %bitcast.27), calls=%async_computation.1 | async-start | bytes 1048576 | tf_op jit(solution)/shard_map/all_to_all | solution.py:97
  19.1 462.7 %all-gather.6.cloned.1.call-start = ((), (), s32[]{:S(2)}) async-start(), calls=%async_computation.6 | async-start | bytes 6684672 | tf_op jit(solution)/shard_map/all_gather | solution.py:89
  101.5 7.4 %copy-start.4 = (s32[1,3072]{1,0:T(1,128)S(1)}, s32[1,3072]{1,0:T(1,128)}, u32[]{:S(2)}) copy-start(s32[1,3072]{1,0:T(1,128)} %param.11) | copy-start | bytes 36868
  101.5 35.7 %all-to-all-start = ((bf16[192,16,192]{2,0,1:T(8,128)(2,1)}), bf16[192,16,192]{2,0,1:T(8,128)(2,1)S(1)}, u32[]{:S(2)}, u32[]{:S(2)}) async-start(bf16[192,16,192]{2,0,1:T(8,128)(2,1)} %copy.93), calls=%async_computation | async-start | bytes 3145728 | tf_op jit(solution)/shard_map/all_to_all | solution.py:96
  155.4 1.0 copy-start
  203.2 1.0 copy-start
  250.9 1.0 copy-start
  298.6 1.0 copy-start
  346.3 1.0 copy-start
  394.0 1.0 copy-start
  437.8 1.1 copy-start.1
  448.6 8.6 %copy-start.2 = (bf16[1,48,64,64]{3,2,1,0:T(8,128)(2,1)S(1)}, bf16[1,48,64,64]{3,2,1,0:T(8,128)(2,1)}, u32[]{:S(2)}) copy-start(bf16[1,48,64,64]{3,2,1,0:T(8,128)(2,1)} %convert_element_type.62) | copy-start | bytes 1179652
  451.4 23.1 %all-to-all-start.2 = ((bf16[16,2,6144]{2,1,0:T(2,128)(2,1)}), bf16[16,2,6144]{2,1,0:T(2,128)(2,1)S(1)}, u32[]{:S(2)}, u32[]{:S(2)}) async-start(bf16[16,2,6144]{2,1,0:T(2,128)(2,1)} %reshape.322), calls=%async_computation.2 | async-start | bytes 786432 | tf_op jit(solution)/shard_map/all_to_all | solution.py:120
  474.5 119.7 %all-to-all-start.3 = ((bf16[16,2,18432]{2,1,0:T(2,128)(2,1)}), bf16[16,2,18432]{2,1,0:T(2,128)(2,1)}, u32[]{:S(2)}, u32[]{:S(2)}) async-start(bf16[16,2,18432]{2,1,0:T(2,128)(2,1)} %reshape.324), calls=%async_computation.3 | async-start | bytes 2359296 | tf_op jit(solution)/shard_map/all_to_all | solution.py:121
  481.7 110.9 %reduce-scatter.4.cloned.1.call-start = ((), (), s32[]{:S(2)}) async-start(), calls=%async_computation.7 | async-start | bytes 540672
Sparse Core Ops, SparseCore 0:
  10.2 81.2 all-gather.3
  94.5 83.8 all-gather.5
  487.2 105.4 reduce-scatter.3
where the time goes:
time: 633 us; the launch traced here: 628 us
  waiting for transfers between devices  178 us (28%)
  matrix products  168 us (27%)
  local copies, waits for them, and re-layouts  140 us (22%)
  other arithmetic  99 us (16%)
  starting transfers between devices  29.8 us (5%)
  between operations  14 us (2%)
    unnamed x4, waiting for transfers between devices  103 us
    all_gather x1, waiting for transfers between devices, per_device(): weights_all = lax.all_gather(qkv_weight, 'dp', axis=0, tiled=True)  70.2 us
    reshape x6, matrix products, group_step(): key_terms.reshape(in_group, slot_count, block_rows, head_width)  42.2 us
    scatter-add x6, other arithmetic, group_step(): grad_value.at[block_ids]  42 us
    scatter-add x6, other arithmetic, group_step(): grad_key.at[block_ids]  42 us
    dot_general x6, matrix products, group_step(): jnp.einsum('cqk,cke->cqe', grad_scores, key_rows, preferred_element_type=...  36 us
    reshape x6, matrix products, group_step(): value_terms.reshape(in_group, slot_count, block_rows, head_width)  25.7 us
    dot_general x6, matrix products, group_step(): jnp.einsum('cqk,cke->cqe', attn_low, value_rows, preferred_element_type=j...  21 us
  transfers between devices with their start and end apart: 7, of which 3 were waited for; matrix products, arithmetic and copies ran while one was open for 59% of the time, Pallas kernels for 0%

commit v1 on v0

--- a/solution.py
+++ b/solution.py
@@ -85,7 +85,9 @@
     three_width = 3 * HD
     node_feats = features[0]
     cot_heads = cotangent[0].reshape(local_rows, HEADS, HD)
-    weights_all = lax.all_gather(qkv_weight, "dp", axis=0, tiled=True)
+    weights_all = jnp.concatenate(
+        lax.all_to_all(jnp.stack([qkv_weight] * lax.axis_size("dp")), "dp", 0, 0), axis=0
+    )
     node_all = lax.all_gather(node_feats, "seq", axis=0, tiled=True)
     node_count = node_all.shape[0]
     projected = jnp.dot(node_feats, weights_all, preferred_element_type=jnp.float32).astype(

time: 633 us -> 847 us (1.34)
  the two profiles are of different devices: /device:TPU:8 before, /device:TPU:2 now
where the time goes in v1:
time: 847 us; the launch traced here: 843 us
  waiting for transfers between devices  374 us (44%)
  matrix products  168 us (20%)
  local copies, waits for them, and re-layouts  143 us (17%)
  other arithmetic  99 us (12%)
  starting transfers between devices  44.7 us (5%)
  between operations  14.3 us (2%)
    all_to_all x1, waiting for transfers between devices, per_device(): lax.all_to_all(jnp.stack([qkv_weight] * lax.axis_size('dp')), 'dp', 0, 0)  272 us
    unnamed x3, waiting for transfers between devices  101 us
    reshape x6, matrix products, group_step(): key_terms.reshape(in_group, slot_count, block_rows, head_width)  42.2 us
    scatter-add x6, other arithmetic, group_step(): grad_value.at[block_ids]  42 us
    scatter-add x6, other arithmetic, group_step(): grad_key.at[block_ids]  42 us
    dot_general x6, matrix products, group_step(): jnp.einsum('cqk,cke->cqe', grad_scores, key_rows, preferred_element_type=...  36 us
    reshape x6, matrix products, group_step(): value_terms.reshape(in_group, slot_count, block_rows, head_width)  25.7 us
    dot_general x6, matrix products, group_step(): jnp.einsum('cqk,cke->cqe', attn_low, value_rows, preferred_element_type=j...  21 us
  transfers between devices with their start and end apart: 7, of which 3 were waited for; matrix products, arithmetic and copies ran while one was open for 44% of the time, Pallas kernels for 0%

profile of v1, /device:TPU:2, one launch (start us, length us, event | category | flops | bytes accessed | tf_op | source)
XLA Modules:
  0.0 842.5 jit_solution(5541352876828276165)
XLA Ops:
  7.2 4.3 stack.2
  11.5 15.7 %all-to-all-start = ((bf16[32,32,3072]{2,1,0:T(8,128)(2,1)}), bf16[32,32,3072]{2,1,0:T(8,128)(2,1)}, u32[]{:S(2)}, u32[]{:S(2)}) async-start(bf16[32,32,3072]{2,1,0:T(8,128)(2,1)} %stack.2), calls=%async_computation | async-start | bytes 12582912 | tf_op jit(solution)/shard_map/all_to_all | solution.py:89
  30.3 271.8 %all-to-all-done = bf16[32,32,3072]{2,1,0:T(8,128)(2,1)} async-done(((bf16[32,32,3072]{2,1,0:T(8,128)(2,1)}), bf16[32,32,3072]{2,1,0:T(8,128)(2,1)}, u32[]{:S(2)}, u32[]{:S(2)}) %all-to-all-start) | async-done | bytes 6291488 | tf_op jit(solution)/shard_map/all_to_all | solution.py:89
  302.2 7.5 all-to-all-start.2
  309.7 5.3 convolution_convert_fusion.2
  314.9 3.0 reshape.202
  320.0 7.0 all-to-all-start.1
  327.1 12.0 %scatter_custom_fusion.2 = s32[3072]{0:T(1024)S(1)} fusion(s32[3072]{0:T(1024)S(1)} %bitcast.183, s32[3072]{0:T(1024)S(1)} %iota.7, s32[]{:T(128)} %copy.139), kind=kCustom, calls=%fused_computation.71 | custom fusion | bytes 12292 | tf_op jit(solution)/shard_map/scatter | solution.py:105
  339.5 11.4 %gather_fusion.3 = bf16[3072,64]{1,0:T(8,128)(2,1)} fusion(bf16[3072,64]{1,0:T(8,128)(2,1)S(1)} %bitcast.162, s32[3072]{0:T(1024)S(1)} %broadcast_clamp_fusion), kind=kCustom, calls=%fused_computation.3 | custom fusion | bytes 798720 | tf_op jit(solution)/shard_map/gather | solution.py:108
  350.9 11.1 %gather_fusion.2 = bf16[3072,192]{1,0:T(8,128)(2,1)S(1)} fusion(bf16[3072,192]{1,0:T(8,128)(2,1)S(1)} %bitcast.153, s32[3072]{0:T(1024)S(1)} %broadcast_clamp_fusion), kind=kCustom, calls=%fused_computation.2 | custom fusion | bytes 2371584 | tf_op jit(solution)/shard_map/gather | solution.py:107
  364.1 286.3 %while.16 = (s32[]{:T(128)}, f32[1,48,64,64]{3,2,1,0:T(8,128)S(1)}, f32[1,48,64,64]{3,2,1,0:T(8,128)S(1)}, bf16[6,1,8,64,64]{4,3,2,1,0:T(8,128)(2,1)}, bf16[6,1,...) while((s32[]{:T(128)}, f32[1,48,64,64]{3,2,1,0:T(8,128)S(1)}, ...), condition=%wide.region_6.7_spmd, body=%wide.region_0.6_spmd.sunk | while | flops 209000192 | bytes 36499064 | solution.py:70
  364.2 2.9 gather_fusion.1
  377.0 6.0 fusion.113
  383.0 4.3 fusion.111
  387.3 7.0 scatter_fusion.1
  394.3 7.0 fusion.110
  401.3 7.0 scatter_fusion
  408.3 3.5 fusion.112
  411.9 2.9 gather_fusion.1
  424.7 6.0 fusion.113
  430.7 4.3 fusion.111
  435.0 7.0 scatter_fusion.1
  442.0 7.0 fusion.110
  449.0 7.0 scatter_fusion
  456.1 3.5 fusion.112
  459.7 2.9 gather_fusion.1
  472.4 6.0 fusion.113
  478.4 4.3 fusion.111
  482.7 7.0 scatter_fusion.1
  489.7 7.0 fusion.110
  496.8 7.0 scatter_fusion
  503.8 3.5 fusion.112
  507.4 2.9 gather_fusion.1
  520.2 6.0 fusion.113
  526.2 4.3 fusion.111
  530.4 7.0 scatter_fusion.1
  537.4 7.0 fusion.110
  544.5 7.0 scatter_fusion
  551.5 3.5 fusion.112
  555.1 2.9 gather_fusion.1
  565.0 2.8 fusion.106
  567.9 6.0 fusion.113
  573.9 4.3 fusion.111
  578.1 7.0 scatter_fusion.1
  585.2 7.0 fusion.110
  592.2 7.0 scatter_fusion
  599.2 3.5 fusion.112
  602.8 2.9 gather_fusion.1
  615.6 6.0 fusion.113
  621.6 4.3 fusion.111
  625.9 7.0 scatter_fusion.1
  632.9 7.0 fusion.110
  639.9 7.0 scatter_fusion
  646.9 3.5 fusion.112
  652.6 9.2 %gather_fusion.4 = bf16[3072,64]{1,0:T(8,128)(2,1)S(1)} fusion(bf16[3072,64]{1,0:T(8,128)(2,1)S(1)} %bitcast.165, s32[3072]{0:T(1024)S(1)} %fusion.52), kind=kCustom, calls=%fused_computation.4 | custom fusion | bytes 798720 | tf_op jit(solution)/shard_map/gather | solution.py:120
  665.1 7.2 all-to-all-start.3
  674.2 11.1 %gather_fusion.5 = bf16[3072,192]{1,0:T(8,128)(2,1)S(1)} fusion(bf16[3072,192]{1,0:T(8,128)(2,1)S(1)} %maximum_bitcast_fusion, s32[3072]{0:T(1024)S(1)} %fusion.52), kind=kCustom, calls=%fused_computation.5 | custom fusion | bytes 2371584 | tf_op jit(solution)/shard_map/gather | solution.py:119
  689.5 7.2 all-to-all-start.4
  696.8 4.2 fusion.48
  706.1 100.7 %reduce-scatter.4.cloned.1.call-done = bf16[32,192]{1,0:T(8,128)(2,1)} async-done(((bf16[1024,192]{1,0:T(8,128)(2,1)}), bf16[32,192]{1,0:T(8,128)(2,1)}) %reduce-scatter.4.cloned.1.call-update) | async-done | bytes 12304
  808.4 8.4 reshape.331
  816.7 6.2 copy.102
  822.9 3.0 all_to_all.64
  829.9 5.7 fusion.47
  (134 shorter events, 87.0 us)
Async XLA Ops:
  11.5 16.5 %copy-start.3 = (bf16[1,192,1024]{2,1,0:T(8,128)(2,1)S(1)}, bf16[1,192,1024]{2,1,0:T(8,128)(2,1)}, u32[]{:S(2)}) copy-start(bf16[1,192,1024]{2,1,0:T(8,128)(2,1)} %param.10) | copy-start | bytes 1179652
  11.5 17.5 %copy-start.6 = (s32[1,48,8]{1,2,0:T(8,128)S(1)}, s32[1,48,8]{1,2,0:T(8,128)}, u32[]{:S(2)}) copy-start(s32[1,48,8]{1,2,0:T(8,128)} %param.12) | copy-start | bytes 4612
  11.5 18.1 %copy-start.7 = (s32[1,48]{1,0:T(1,128)S(1)}, s32[1,48]{1,0:T(1,128)}, u32[]{:S(2)}) copy-start(s32[1,48]{1,0:T(1,128)} %param.13) | copy-start | bytes 580
  11.5 290.7 %all-to-all-start = ((bf16[32,32,3072]{2,1,0:T(8,128)(2,1)}), bf16[32,32,3072]{2,1,0:T(8,128)(2,1)}, u32[]{:S(2)}, u32[]{:S(2)}) async-start(bf16[32,32,3072]{2,1,0:T(8,128)(2,1)} %stack.2), calls=%async_computation | async-start | bytes 12582912 | tf_op jit(solution)/shard_map/all_to_all | solution.py:89
  27.2 282.4 %copy-start.4 = (bf16[1,192,1024]{2,1,0:T(8,128)(2,1)S(1)}, bf16[1,192,1024]{2,1,0:T(8,128)(2,1)}, u32[]{:S(2)}) copy-start(bf16[1,192,1024]{2,1,0:T(8,128)(2,1)} %param.8) | copy-start | bytes 1179652
  27.2 669.6 %all-gather.3.cloned.1.call-start = ((), (), s32[]{:S(2)}) async-start(), calls=%async_computation.6 | async-start | bytes 6684672 | tf_op jit(solution)/shard_map/all_gather | solution.py:91
  302.2 17.8 %all-to-all-start.2 = ((bf16[192,16,64]{0,2,1:T(8,128)(2,1)}), bf16[192,16,64]{0,2,1:T(8,128)(2,1)S(1)}, u32[]{:S(2)}, u32[]{:S(2)}) async-start(bf16[192,16,64]{0,2,1:T(8,128)(2,1)} %bitcast.28), calls=%async_computation.2 | async-start | bytes 1048576 | tf_op jit(solution)/shard_map/all_to_all | solution.py:99
  319.7 7.4 copy-start.5
  320.0 30.9 %all-to-all-start.1 = ((bf16[192,16,192]{2,0,1:T(8,128)(2,1)}), bf16[192,16,192]{2,0,1:T(8,128)(2,1)S(1)}, u32[]{:S(2)}, u32[]{:S(2)}) async-start(bf16[192,16,192]{2,0,1:T(8,128)(2,1)} %copy.93), calls=%async_computation.1 | async-start | bytes 3145728 | tf_op jit(solution)/shard_map/all_to_all | solution.py:98
  369.1 1.0 copy-start
  416.9 1.0 copy-start
  464.6 1.0 copy-start
  512.3 1.0 copy-start
  560.0 1.0 copy-start
  607.7 1.0 copy-start
  651.5 1.1 copy-start.1
  662.3 10.0 %copy-start.2 = (bf16[1,48,64,64]{3,2,1,0:T(8,128)(2,1)S(1)}, bf16[1,48,64,64]{3,2,1,0:T(8,128)(2,1)}, u32[]{:S(2)}) copy-start(bf16[1,48,64,64]{3,2,1,0:T(8,128)(2,1)} %convert_element_type.62) | copy-start | bytes 1179652
  665.1 24.5 %all-to-all-start.3 = ((bf16[16,2,6144]{2,1,0:T(2,128)(2,1)}), bf16[16,2,6144]{2,1,0:T(2,128)(2,1)S(1)}, u32[]{:S(2)}, u32[]{:S(2)}) async-start(bf16[16,2,6144]{2,1,0:T(2,128)(2,1)} %reshape.328), calls=%async_computation.3 | async-start | bytes 786432 | tf_op jit(solution)/shard_map/all_to_all | solution.py:122
  689.5 118.8 %all-to-all-start.4 = ((bf16[16,2,18432]{2,1,0:T(2,128)(2,1)}), bf16[16,2,18432]{2,1,0:T(2,128)(2,1)}, u32[]{:S(2)}, u32[]{:S(2)}) async-start(bf16[16,2,18432]{2,1,0:T(2,128)(2,1)} %reshape.330), calls=%async_computation.4 | async-start | bytes 2359296 | tf_op jit(solution)/shard_map/all_to_all | solution.py:123
  696.8 110.1 %reduce-scatter.4.cloned.1.call-start = ((), (), s32[]{:S(2)}) async-start(), calls=%async_computation.7 | async-start | bytes 540672
Sparse Core Ops, SparseCore 0:
  31.1 77.5 all-gather.2
  702.2 104.5 reduce-scatter.3
